TPU v7x, 32 devices: a whole 2x2x4 slice. The times are simulated.
32 devices in a mesh: tp: 4 (over y, x), row: 4 (over z), col: 2 (over core).
Axes of the slice: x: 2, y: 2, z: 4, core: 2. Of those that a mesh axis runs over, the one named last changes fastest.
Arguments:
- hidden: bfloat16 [128, 14336], P('col', 'row'), may hold values from -6 to 6
- out_grad: bfloat16 [128, 4096], P(None, ('tp', 'row')), may hold values from -6 to 6
- basis_in: bfloat16 [14336, 4096], P(('row', 'col'), 'tp'), may hold values from -0.046875 to 0.046875
- basis_out: bfloat16 [4096, 1024], P(('tp', 'row'), 'col'), may hold values from -0.09375 to 0.09375
- eigen: float32 [4096, 1024], P(('tp', 'row'), 'col'), may hold values from 0.02 to 2
Outputs:
- precond: float32 [4096, 14336], P(('tp', 'col'), 'row')
All inputs are finite; a program needn't handle non-finite values.
Results may differ from a plain program's by a relative error of at most 0.024.
Values may be sent and summed in bfloat16 or wider, within the bound.
No kernel may reach another device: no remote copies, remote signals or barrier semaphores. Data moves between devices by JAX's collectives and lax.ppermute only.
A program may use at most 64 MiB of HBM per device.

v0:
```python
import jax
import jax.numpy as jnp
from jax import lax
from jax.sharding import PartitionSpec as P

damping = 0.01


def contract_rows(left, right):
    return lax.dot_general(
        left, right, (((0,), (0,)), ((), ())), preferred_element_type=jnp.float32
    )


def contract_cols(left, right):
    return lax.dot_general(
        left, right, (((1,), (1,)), ((), ())), preferred_element_type=jnp.float32
    )


def shards(hidden, out_grad, basis_in, basis_out, eigen):
    tp_count = lax.axis_size("tp")
    col_count = lax.axis_size("col")
    basis_block = lax.all_gather(basis_in, "col", axis=0, tiled=True)
    partial_in = jnp.dot(hidden, basis_block, preferred_element_type=jnp.float32)
    rotated_in = lax.psum_scatter(
        partial_in.astype(jnp.bfloat16), "row", scatter_dimension=1, tiled=True
    )
    rotated_in = lax.all_gather(rotated_in, "col", axis=0, tiled=True)
    queries = rotated_in.shape[0]
    partial_out = jnp.dot(out_grad, basis_out, preferred_element_type=jnp.float32)
    rotated_out = lax.psum(partial_out, ("tp", "row")).astype(jnp.bfloat16)
    coeff = contract_rows(rotated_in, rotated_out)
    scaled = (coeff / (queries * (eigen + damping))).astype(jnp.bfloat16)
    mixed_part = contract_cols(scaled, lax.all_gather(basis_out, ("tp", "row"), axis=0, tiled=True))
    depth = mixed_part.shape[0]
    width = mixed_part.shape[1]
    mixed_part = mixed_part.reshape(depth, tp_count, col_count, width // (tp_count * col_count))
    mixed = lax.psum_scatter(
        mixed_part.astype(jnp.bfloat16), "col", scatter_dimension=2, tiled=True
    ).astype(jnp.float32)
    mixed = mixed.reshape(depth, width // col_count).astype(jnp.bfloat16)
    mixed = lax.all_gather(mixed, "row", axis=0, tiled=True)
    return lax.psum_scatter(
        lax.dot_general(
            mixed, basis_block, (((0,), (1,)), ((), ())), preferred_element_type=jnp.float32
        ).astype(jnp.bfloat16),
        "tp",
        scatter_dimension=0,
        tiled=True,
    ).astype(jnp.float32)


def solution(mesh):
    placed = (
        P("col", "row"),
        P(None, ("tp", "row")),
        P(("row", "col"), "tp"),
        P(("tp", "row"), "col"),
        P(("tp", "row"), "col"),
    )
    return jax.shard_map(
        shards, mesh=mesh, in_specs=placed, out_specs=P(("tp", "col"), "row"), check_vma=False
    )
```

profile of v0, /device:TPU:0, one launch (start us, length us, event | category | flops | bytes accessed | tf_op | source)
XLA Modules:
  0.0 397.8 jit_solution(9604397828768367093)
XLA Ops:
  7.4 0.0 copy-start
  7.4 0.0 all-gather.4.cloned.1.call-start
  7.4 0.7 all-gather.4.cloned.1.call-update
  8.1 0.0 copy-start.1
  8.1 0.0 copy-start.2
  8.1 0.0 copy-start.3
  8.1 0.0 reduce-scatter.4.cloned.1.call-start
  8.2 22.6 %all-gather.4.cloned.1.call-done = bf16[3584,1024]{1,0:T(8,128)(2,1)} async-done(((bf16[1792,1024]{1,0:T(8,128)(2,1)}), bf16[3584,1024]{1,0:T(8,128)(2,1)}) %all-gather.4.cloned.1.call-update) | async-done | bytes 7340048 | tf_op jit(solution)/shard_map/all_gather | solution.py:24
  30.8 0.0 copy-done
  30.8 5.1 %convolution_convert_fusion.2 = bf16[64,1024]{1,0:T(8,128)(2,1)} fusion(bf16[64,3584]{1,0:T(8,128)(2,1)S(1)} %copy-done, bf16[3584,1024]{1,0:T(8,128)(2,1)} %all-gather.4.cloned.1.call-done), kind=kOutput, calls=%fused_computation.4 | convolution fusion | flops 469827584 | bytes 7929856 | tf_op jit(solution)/shard_map/dot_general | solution.py:25
  35.9 0.0 reduce-scatter.4.cloned.1.call-update
  35.9 0.0 all-gather.6.cloned.1.call-start
  36.0 0.5 all-gather.6.cloned.1.call-update
  36.5 0.0 reduce-scatter.6.cloned.1.call-start
  36.5 0.0 copy-done.1
  36.6 0.0 copy-done.2
  36.6 0.2 fusion.9
  36.8 85.1 %all-reduce.1 = bf16[128,512]{1,0:T(8,128)(2,1)S(1)} all-reduce(f32[128,512]{1,0:T(8,128)S(1)} %fusion.9), channel_id=1, replica_groups=mesh['tp'=4,'row'=4,'col'=2] {'tp','row'}, use_global_device_ids=true, to_apply=%region_1.0 | all-reduce | flops 65536 | bytes 393216 | tf_op jit(solution)/shard_map/psum | solution.py:32
  121.9 0.0 reduce-scatter.4.cloned.1.call-done
  121.9 2.1 all_gather.13
  124.0 0.0 all-gather.6.cloned.1.call-done
  124.0 0.0 copy-done.3
  124.0 4.9 %convolution_convert_fusion.1 = bf16[256,4096]{1,0:T(8,128)(2,1)} fusion(bf16[4096,512]{1,0:T(8,128)(2,1)} %all-gather.6.cloned.1.call-done, bf16[128,256]{1,0:T(8,128)(2,1)S(1)} %all_gather.13, f32[256,512]{1,0:T(8,128)S(1)} %copy-done.3, bf16[128,512]{1,0:T(8,128)(2,1)S(1)} %all-reduce.1), kind=kOutput, calls=%fused_computation.1 | convolution fusion | flops 1108869120 | bytes 7012352 | tf_op jit(solution)/shard_map/dot_general | solution.py:16
  128.9 3.3 convert_element_type.30
  132.2 4.1 %copy.6 = bf16[256,4,2,512]{0,3,1,2:T(8,128)(2,1)} copy(bf16[256,4,2,512]{3,2,1,0:T(2,128)(2,1)S(1)} %convert_element_type.30) | data formatting | bytes 4194304 | tf_op jit(solution)/shard_map/convert_element_type | solution.py:40
  136.3 0.0 reduce-scatter.6.cloned.1.call-update
  136.4 0.0 all-gather.8.cloned.1.call-start
  136.4 6.9 %reduce-scatter.6.cloned.1.call-done = bf16[256,4,1,512]{0,3,1,2:T(8,128)(2,1)} async-done(((bf16[256,4,2,512]{0,3,1,2:T(8,128)(2,1)}), bf16[256,4,1,512]{0,3,1,2:T(8,128)(2,1)}) %reduce-scatter.6.cloned.1.call-update) | async-done | bytes 1048592 | tf_op jit(solution)/shard_map/reduce_scatter | solution.py:39
  143.3 0.0 all-gather.8.cloned.1.call-update
  143.4 0.0 reduce-scatter.8.cloned.1.call-start
  143.4 83.2 %all-gather.8.cloned.1.call-done = bf16[1024,2048]{0,1:T(8,128)(2,1)} async-done(((bf16[256,2048]{0,1:T(8,128)(2,1)}), bf16[1024,2048]{0,1:T(8,128)(2,1)}) %all-gather.8.cloned.1.call-update) | async-done | bytes 4194320 | tf_op jit(solution)/shard_map/all_gather | solution.py:43
  226.6 22.0 %convolution_convert_fusion = bf16[2048,3584]{1,0:T(8,128)(2,1)} fusion(bf16[1024,2048]{0,1:T(8,128)(2,1)} %all-gather.8.cloned.1.call-done, bf16[3584,1024]{1,0:T(8,128)(2,1)} %all-gather.4.cloned.1.call-done), kind=kOutput, calls=%fused_computation | convolution fusion | flops 15039725568 | bytes 26214400 | tf_op jit(solution)/shard_map/dot_general | solution.py:45
  248.6 0.0 reduce-scatter.8.cloned.1.call-update
  248.7 135.9 %reduce-scatter.8.cloned.1.call-done = bf16[512,3584]{1,0:T(8,128)(2,1)} async-done(((bf16[2048,3584]{1,0:T(8,128)(2,1)}), bf16[512,3584]{1,0:T(8,128)(2,1)}) %reduce-scatter.8.cloned.1.call-update) | async-done | bytes 3670032 | tf_op jit(solution)/shard_map/reduce_scatter | solution.py:44
  384.6 6.0 %convert_element_type.33 = f32[512,3584]{1,0:T(8,128)} convert(bf16[512,3584]{1,0:T(8,128)(2,1)} %reduce-scatter.8.cloned.1.call-done) | non-fusion elementwise | flops 1835008 | bytes 11010048 | tf_op jit(solution)/shard_map/convert_element_type | solution.py:51
Async XLA Ops:
  7.4 23.4 %copy-start = (bf16[64,3584]{1,0:T(8,128)(2,1)S(1)}, bf16[64,3584]{1,0:T(8,128)(2,1)}, u32[]{:S(2)}) copy-start(bf16[64,3584]{1,0:T(8,128)(2,1)} %param.5) | copy-start | bytes 1376260
  7.4 23.4 %all-gather.4.cloned.1.call-start = ((), (), s32[]{:S(2)}) async-start(), calls=%async_computation.3 | async-start | bytes 11010048 | tf_op jit(solution)/shard_map/all_gather | solution.py:24
  8.1 28.5 %copy-start.1 = (bf16[256,512]{1,0:T(8,128)(2,1)S(1)}, bf16[256,512]{1,0:T(8,128)(2,1)}, u32[]{:S(2)}) copy-start(bf16[256,512]{1,0:T(8,128)(2,1)} %param.8) | copy-start | bytes 786436
  8.1 28.5 %copy-start.2 = (bf16[128,256]{1,0:T(8,128)(2,1)S(1)}, bf16[128,256]{1,0:T(8,128)(2,1)}, u32[]{:S(2)}) copy-start(bf16[128,256]{1,0:T(8,128)(2,1)} %param.6) | copy-start | bytes 196612
  8.1 115.9 %copy-start.3 = (f32[256,512]{1,0:T(8,128)S(1)}, f32[256,512]{1,0:T(8,128)}, u32[]{:S(2)}) copy-start(f32[256,512]{1,0:T(8,128)} %param.9) | copy-start | bytes 1572868
  8.1 113.8 %reduce-scatter.4.cloned.1.call-start = ((), (), s32[]{:S(2)}) async-start(), calls=%async_computation.4 | async-start | bytes 163840 | tf_op jit(solution)/shard_map/reduce_scatter | solution.py:26
  35.9 88.1 %all-gather.6.cloned.1.call-start = ((), (), s32[]{:S(2)}) async-start(), calls=%async_computation.5 | async-start | bytes 4456448 | tf_op jit(solution)/shard_map/all_gather | solution.py:35
  36.5 106.8 %reduce-scatter.6.cloned.1.call-start = ((), (), s32[]{:S(2)}) async-start(), calls=%async_computation.6 | async-start | bytes 3145728 | tf_op jit(solution)/shard_map/reduce_scatter | solution.py:39
  136.4 90.2 %all-gather.8.cloned.1.call-start = ((), (), s32[]{:S(2)}) async-start(), calls=%async_computation.7 | async-start | bytes 5242880 | tf_op jit(solution)/shard_map/all_gather | solution.py:43
  143.4 241.2 %reduce-scatter.8.cloned.1.call-start = ((), (), s32[]{:S(2)}) async-start(), calls=%async_computation.8 | async-start | bytes 18350080 | tf_op jit(solution)/shard_map/reduce_scatter | solution.py:44
Sparse Core Ops, SparseCore 0:
  9.7 21.0 all-gather.3
  36.0 21.2 reduce-scatter.3
  136.5 6.8 reduce-scatter.5
  144.7 81.7 all-gather.7
Sparse Core Ops, SparseCore 1:
  39.2 78.1 all-gather.5
  248.7 135.8 reduce-scatter.7
where the time goes:
time: 398 us
  waiting for transfers between devices  250 us (63%)
  blocking collectives  87.2 us (22%)
  matrix products  32.3 us (8%)
  between operations  14.7 us (4%)
  local copies, waits for them, and re-layouts  7.4 us (2%)
  other arithmetic  6.04 us (2%)
    reduce_scatter x1, waiting for transfers between devices, shards(): lax.psum_scatter(lax.dot_general(mixed, basis_block, (((0,), (1,)), ((),...  136 us
    psum x1, blocking collectives, shards(): rotated_out = lax.psum(partial_out, ('tp', 'row')).astype(jnp.bfloat16)  85.1 us
    all_gather x1, waiting for transfers between devices, shards(): mixed = lax.all_gather(mixed, 'row', axis=0, tiled=True)  83.2 us
    all_gather x1, waiting for transfers between devices, shards(): basis_block = lax.all_gather(basis_in, 'col', axis=0, tiled=True)  22.6 us
    dot_general x1, matrix products, shards(): lax.dot_general(mixed, basis_block, (((0,), (1,)), ((), ())), preferred_e...  22 us
  transfers between devices with their start and end apart: 6, of which 4 were waited for; matrix products, arithmetic and copies ran while one was open for 0% of the time, Pallas kernels for 0%

commit v1 on v0

--- a/solution.py
+++ b/solution.py
@@ -40,7 +40,12 @@
         mixed_part.astype(jnp.bfloat16), "col", scatter_dimension=2, tiled=True
     ).astype(jnp.float32)
     mixed = mixed.reshape(depth, width // col_count).astype(jnp.bfloat16)
-    mixed = lax.all_gather(mixed, "row", axis=0, tiled=True)
+    by_rank = []
+    for _ in range(lax.axis_size("row")):
+        by_rank.append(mixed)
+    state_now = jnp.stack(by_rank, axis=0)
+    val = lax.all_to_all(state_now, "row", 0, 0)
+    mixed = jnp.concatenate(val, 0)
     return lax.psum_scatter(
         lax.dot_general(
             mixed, basis_block, (((0,), (1,)), ((), ())), preferred_element_type=jnp.float32

time: 398 us -> 415 us (1.043)
  blocking collectives: 87.2 us -> 185 us
  waiting for transfers between devices: 250 us -> 168 us
    all_to_all x0 -> x1, blocking collectives: none -> 98.2 us  [shards(): val = lax.all_to_all(state_now, 'row', 0, 0)]
    all_gather x1 -> x0, waiting for transfers between devices: 83.2 us -> none  [shards(): mixed = lax.all_gather(mixed, 'row', axis=0, tiled=True)]
  transfers between devices with their start and end apart: 6 -> 5, of which waited for: 4 -> 3; matrix products, arithmetic and copies ran while one was open for 0% -> 0% of each run, Pallas kernels for 0% -> 0%
where the time goes in v1:
time: 415 us
  blocking collectives  185 us (45%)
  waiting for transfers between devices  168 us (40%)
  matrix products  31.4 us (8%)
  between operations  14.7 us (4%)
  local copies, waits for them, and re-layouts  9.4 us (2%)
  other arithmetic  6.04 us (1%)
    reduce_scatter x1, waiting for transfers between devices, shards(): lax.psum_scatter(lax.dot_general(mixed, basis_block, (((0,), (1,)), ((),...  137 us
    all_to_all x1, blocking collectives, shards(): val = lax.all_to_all(state_now, 'row', 0, 0)  98.2 us
    psum x1, blocking collectives, shards(): rotated_out = lax.psum(partial_out, ('tp', 'row')).astype(jnp.bfloat16)  85.1 us
    all_gather x1, waiting for transfers between devices, shards(): basis_block = lax.all_gather(basis_in, 'col', axis=0, tiled=True)  22.6 us
    dot_general x1, matrix products, shards(): lax.dot_general(mixed, basis_block, (((0,), (1,)), ((), ())), preferred_e...  21.2 us
  transfers between devices with their start and end apart: 5, of which 3 were waited for; matrix products, arithmetic and copies ran while one was open for 0% of the time, Pallas kernels for 0%

profile of v1, /device:TPU:0, one launch (start us, length us, event | category | flops | bytes accessed | tf_op | source)
XLA Modules:
  0.0 414.7 jit_solution(7085943840375429739)
XLA Ops:
  7.4 0.0 copy-start
  7.4 0.0 all-gather.3.cloned.1.call-start
  7.4 0.7 all-gather.3.cloned.1.call-update
  8.1 0.0 copy-start.1
  8.1 0.0 copy-start.2
  8.1 0.0 copy-start.3
  8.1 0.0 reduce-scatter.4.cloned.1.call-start
  8.2 22.6 %all-gather.3.cloned.1.call-done = bf16[3584,1024]{1,0:T(8,128)(2,1)} async-done(((bf16[1792,1024]{1,0:T(8,128)(2,1)}), bf16[3584,1024]{1,0:T(8,128)(2,1)}) %all-gather.3.cloned.1.call-update) | async-done | bytes 7340048 | tf_op jit(solution)/shard_map/all_gather | solution.py:24
  30.8 0.0 copy-done
  30.8 5.1 %convolution_convert_fusion.2 = bf16[64,1024]{1,0:T(8,128)(2,1)} fusion(bf16[64,3584]{1,0:T(8,128)(2,1)S(1)} %copy-done, bf16[3584,1024]{1,0:T(8,128)(2,1)} %all-gather.3.cloned.1.call-done), kind=kOutput, calls=%fused_computation.4 | convolution fusion | flops 469827584 | bytes 7929856 | tf_op jit(solution)/shard_map/dot_general | solution.py:25
  35.9 0.0 reduce-scatter.4.cloned.1.call-update
  35.9 0.0 all-gather.5.cloned.1.call-start
  36.0 0.5 all-gather.5.cloned.1.call-update
  36.5 0.0 reduce-scatter.6.cloned.1.call-start
  36.5 0.0 copy-done.1
  36.6 0.0 copy-done.2
  36.6 0.2 fusion.9
  36.8 85.1 %all-reduce.1 = bf16[128,512]{1,0:T(8,128)(2,1)S(1)} all-reduce(f32[128,512]{1,0:T(8,128)S(1)} %fusion.9), channel_id=1, replica_groups=mesh['tp'=4,'row'=4,'col'=2] {'tp','row'}, use_global_device_ids=true, to_apply=%region_1.0 | all-reduce | flops 65536 | bytes 393216 | tf_op jit(solution)/shard_map/psum | solution.py:32
  121.9 0.0 reduce-scatter.4.cloned.1.call-done
  121.9 2.1 all_gather.10
  124.0 0.0 all-gather.5.cloned.1.call-done
  124.0 0.0 copy-done.3
  124.0 4.9 %convolution_convert_fusion.1 = bf16[256,4096]{1,0:T(8,128)(2,1)} fusion(bf16[4096,512]{1,0:T(8,128)(2,1)} %all-gather.5.cloned.1.call-done, bf16[128,256]{1,0:T(8,128)(2,1)S(1)} %all_gather.10, f32[256,512]{1,0:T(8,128)S(1)} %copy-done.3, bf16[128,512]{1,0:T(8,128)(2,1)S(1)} %all-reduce.1), kind=kOutput, calls=%fused_computation.1 | convolution fusion | flops 1108869120 | bytes 7012352 | tf_op jit(solution)/shard_map/dot_general | solution.py:16
  128.9 3.3 convert_element_type.32
  132.2 4.1 copy.6
  136.3 0.0 reduce-scatter.6.cloned.1.call-update
  136.4 0.0 reduce-scatter.8.cloned.1.call-start
  136.4 6.9 %reduce-scatter.6.cloned.1.call-done = bf16[256,4,1,512]{0,3,1,2:T(8,128)(2,1)} async-done(((bf16[256,4,2,512]{0,3,1,2:T(8,128)(2,1)}), bf16[256,4,1,512]{0,3,1,2:T(8,128)(2,1)}) %reduce-scatter.6.cloned.1.call-update) | async-done | bytes 1048592 | tf_op jit(solution)/shard_map/reduce_scatter | solution.py:39
  143.3 1.5 copy.7
  144.8 0.5 stack.2
  145.3 98.2 %all_to_all.5 = bf16[4,256,2048]{2,1,0:T(8,128)(2,1)S(1)} all-to-all(bf16[4,256,2048]{2,1,0:T(8,128)(2,1)S(1)} %stack.2), channel_id=1, replica_groups=mesh['tp'=4,'row'=4,'col'=2] {'row'}, dimensions={0} | all-to-all | bytes 8388608 | tf_op jit(solution)/shard_map/all_to_all | solution.py:47
  243.6 21.2 %convolution_convert_fusion = bf16[2048,3584]{1,0:T(8,128)(2,1)} fusion(bf16[1024,2048]{1,0:T(8,128)(2,1)S(1)} %bitcast.11, bf16[3584,1024]{1,0:T(8,128)(2,1)} %all-gather.3.cloned.1.call-done), kind=kOutput, calls=%fused_computation | convolution fusion | flops 15039725568 | bytes 26214400 | tf_op jit(solution)/shard_map/dot_general | solution.py:50
  264.7 0.0 reduce-scatter.8.cloned.1.call-update
  264.8 136.8 %reduce-scatter.8.cloned.1.call-done = bf16[512,3584]{1,0:T(8,128)(2,1)} async-done(((bf16[2048,3584]{1,0:T(8,128)(2,1)}), bf16[512,3584]{1,0:T(8,128)(2,1)}) %reduce-scatter.8.cloned.1.call-update) | async-done | bytes 3670032 | tf_op jit(solution)/shard_map/reduce_scatter | solution.py:49
  401.6 6.0 %convert_element_type.35 = f32[512,3584]{1,0:T(8,128)} convert(bf16[512,3584]{1,0:T(8,128)(2,1)} %reduce-scatter.8.cloned.1.call-done) | non-fusion elementwise | flops 1835008 | bytes 11010048 | tf_op jit(solution)/shard_map/convert_element_type | solution.py:56
Async XLA Ops:
  7.4 23.4 %copy-start = (bf16[64,3584]{1,0:T(8,128)(2,1)S(1)}, bf16[64,3584]{1,0:T(8,128)(2,1)}, u32[]{:S(2)}) copy-start(bf16[64,3584]{1,0:T(8,128)(2,1)} %param.5) | copy-start | bytes 1376260
  7.4 23.4 %all-gather.3.cloned.1.call-start = ((), (), s32[]{:S(2)}) async-start(), calls=%async_computation.4 | async-start | bytes 11010048 | tf_op jit(solution)/shard_map/all_gather | solution.py:24
  8.1 28.5 %copy-start.1 = (bf16[256,512]{1,0:T(8,128)(2,1)S(1)}, bf16[256,512]{1,0:T(8,128)(2,1)}, u32[]{:S(2)}) copy-start(bf16[256,512]{1,0:T(8,128)(2,1)} %param.8) | copy-start | bytes 786436
  8.1 28.5 %copy-start.2 = (bf16[128,256]{1,0:T(8,128)(2,1)S(1)}, bf16[128,256]{1,0:T(8,128)(2,1)}, u32[]{:S(2)}) copy-start(bf16[128,256]{1,0:T(8,128)(2,1)} %param.6) | copy-start | bytes 196612
  8.1 115.9 %copy-start.3 = (f32[256,512]{1,0:T(8,128)S(1)}, f32[256,512]{1,0:T(8,128)}, u32[]{:S(2)}) copy-start(f32[256,512]{1,0:T(8,128)} %param.9) | copy-start | bytes 1572868
  8.1 113.8 %reduce-scatter.4.cloned.1.call-start = ((), (), s32[]{:S(2)}) async-start(), calls=%async_computation.5 | async-start | bytes 163840 | tf_op jit(solution)/shard_map/reduce_scatter | solution.py:26
  35.9 88.1 %all-gather.5.cloned.1.call-start = ((), (), s32[]{:S(2)}) async-start(), calls=%async_computation.6 | async-start | bytes 4456448 | tf_op jit(solution)/shard_map/all_gather | solution.py:35
  36.5 106.8 %reduce-scatter.6.cloned.1.call-start = ((), (), s32[]{:S(2)}) async-start(), calls=%async_computation.7 | async-start | bytes 3145728 | tf_op jit(solution)/shard_map/reduce_scatter | solution.py:39
  136.4 265.2 %reduce-scatter.8.cloned.1.call-start = ((), (), s32[]{:S(2)}) async-start(), calls=%async_computation.8 | async-start | bytes 18350080 | tf_op jit(solution)/shard_map/reduce_scatter | solution.py:49
Sparse Core Ops, SparseCore 0:
  9.7 21.0 all-gather.2
  36.0 21.2 reduce-scatter.3
  136.5 6.8 reduce-scatter.5
Sparse Core Ops, SparseCore 1:
  39.2 78.1 all-gather.4
  264.9 136.6 reduce-scatter.7
